TPU v7x, 32 devices: a whole 2x2x4 slice. The times are simulated.
32 devices in a mesh: tile: 8 (over z, core), layer: 4 (over y, x).
Axes of the slice: x: 2, y: 2, z: 4, core: 2. Of those that a mesh axis runs over, the one named last changes fastest.
Arguments:
- basis: float32 [8, 768, 32], P('tile'), may hold values from -0.21875 to 0.21875
- ranks: int32 [8], P('tile'), may hold values from 8 to 32
- cores: float32 [8, 8, 32, 32], P('tile', 'layer'), may hold values from -1.11 to 1.11
- diag: float32 [8, 768, 768], P('tile', 'layer'), may hold values from 0 to 9, as said below
Outputs:
- factors: float32 [1, 768, 768], P(None, 'layer')
- panel_basis: float32 [1, 768, 32], replicated
- schur_diag: float32 [8, 768, 768], P('tile', 'layer')
- schur_cores: float32 [8, 8, 32, 32], P('tile', 'layer')
Inputs may be any that keep to these rules, and one draw needn't show every extreme that they name: `diag`: each tile is a Gaussian kernel of points in the unit cube plus a multiple of the identity, so symmetric positive definite.
All inputs are finite; a program needn't handle non-finite values.
Results may differ from a plain program's by a relative error of at most 0.0001.
Values sent between devices are 32-bit elements; how exact they have to be, the bound alone decides.
A program may use at most 64 MiB of HBM per device.

v0:
```python
import jax
import jax.numpy as jnp
from jax import lax
from jax.experimental import pallas as pl
from jax.experimental.pallas import tpu as pltpu
from jax.sharding import PartitionSpec as P

HI = lax.Precision.HIGHEST
B = 128
S = 8


def nt(a, b):
    return lax.dot_general(
        a, b, (((1,), (1,)), ((), ())), precision=HI, preferred_element_type=jnp.float32
    )


def nn(a, b):
    return jnp.dot(a, b, precision=HI, preferred_element_type=jnp.float32)


def total(terms):
    while len(terms) > 1:
        terms = [
            terms[i] + terms[i + 1] if i + 1 < len(terms) else terms[i]
            for i in range(0, len(terms), 2)
        ]
    return terms[0]


def spread_lane(block, lane):
    return jnp.broadcast_to(block[:, lane : lane + 1], (S, B))


def spread_row(block, row):
    return jnp.broadcast_to(block[row : row + 1, :], (S, B))


def base_factor(tile_ref, upper_ref, inv_ref):
    groups = B // S
    sub = lax.broadcasted_iota(jnp.int32, (S, B), 0)
    lane = lax.broadcasted_iota(jnp.int32, (S, B), 1)
    left = [tile_ref[S * g : S * g + S, :] for g in range(groups)]
    right = [jnp.where(lane == sub + S * g, 1.0, 0.0) for g in range(groups)]
    for b in range(groups):
        a, q = left[b], right[b]
        cols = [spread_lane(a, S * b + j) for j in range(S)]
        e = [[spread_row(cols[j], i) if j <= i else None for j in range(S)] for i in range(S)]
        inv, low = [], [[None] * S for _ in range(S)]
        for j in range(S):
            inv.append(1.0 / e[j][j])
            for i in range(j + 1, S):
                low[i][j] = e[i][j] * inv[j]
            for k in range(j + 1, S):
                for i in range(k, S):
                    e[i][k] = e[i][k] - low[i][j] * e[k][j]
        ra = [spread_row(a, i) for i in range(S)]
        rq = [spread_row(q, i) for i in range(S)]
        for j in range(S):
            for i in range(j + 1, S):
                ra[i] = ra[i] - low[i][j] * ra[j]
                rq[i] = rq[i] - low[i][j] * rq[j]
        xa, xq = None, None
        for j in range(S):
            root = lax.rsqrt(e[j][j])
            ya, yq = ra[j] * root, rq[j] * root
            xa = ya if xa is None else jnp.where(sub == j, ya, xa)
            xq = yq if xq is None else jnp.where(sub == j, yq, xq)
        upper_ref[S * b : S * b + S, :] = jnp.where(lane >= sub + S * b, xa, 0.0)
        inv_ref[S * b : S * b + S, :] = xq
        if b + 1 == groups:
            break
        wa = [ra[j] * inv[j] for j in range(S)]
        wq = [rq[j] * inv[j] for j in range(S)]
        for i in range(S - 1, 0, -1):
            for j in range(i):
                wa[j] = wa[j] - low[i][j] * wa[i]
                wq[j] = wq[j] - low[i][j] * wq[i]
        for g in range(b + 1, groups):
            m = [spread_lane(left[g], S * b + j) for j in range(S)]
            left[g] = left[g] - total([m[j] * wa[j] for j in range(S)])
            right[g] = right[g] - total([m[j] * wq[j] for j in range(S)])


def chol_kernel(tile_ref, u_ref, lower_ref, z_ref, work, block, upper, inverse):
    order = tile_ref.shape[0]
    panels = order // B
    work[...] = tile_ref[...]
    z_ref[...] = u_ref[...]
    lower_ref[...] = jnp.zeros_like(lower_ref)

    def panel(k, carry):
        at = pl.ds(pl.multiple_of(k * B, B), B)
        block[...] = work[at, at]
        base_factor(block, upper, inverse)
        lower_ref[at, at] = upper[...].T
        z = nn(inverse[...], z_ref[at, :])
        z_ref[at, :] = z
        for c in range(panels - 1):
            @pl.when(k == c)
            def _():
                here = slice(c * B, c * B + B)
                rest = slice(c * B + B, order)
                below = nt(work[rest, here], inverse[...])
                lower_ref[rest, here] = below
                z_ref[rest, :] = z_ref[rest, :] - nn(below, z)
                for j in range(c + 1, panels):
                    cols = slice(j * B, j * B + B)
                    rows = slice(j * B, order)
                    own = below[(j - c - 1) * B :, :]
                    work[rows, cols] = work[rows, cols] - nt(own, own[:B, :])
        return carry

    lax.fori_loop(0, panels, panel, 0)


def factor(tile, panel_u):
    order, rank = panel_u.shape
    vm = pl.BlockSpec(memory_space=pltpu.VMEM)
    return pl.pallas_call(
        chol_kernel,
        out_shape=(
            jax.ShapeDtypeStruct((order, order), jnp.float32),
            jax.ShapeDtypeStruct((order, rank), jnp.float32),
        ),
        in_specs=[vm, vm],
        out_specs=(vm, vm),
        scratch_shapes=[
            pltpu.VMEM((order, order), jnp.float32),
            pltpu.VMEM((B, B), jnp.float32),
            pltpu.VMEM((B, B), jnp.float32),
            pltpu.VMEM((B, B), jnp.float32),
        ],
    )(tile, panel_u)


def broadcast(value, axis, source):
    kept = jnp.where(lax.axis_index(axis) == source, value, 0).astype(value.dtype)
    return lax.psum(kept, axis)


def body(basis, ranks, cores, diag):
    tile_dev = basis.shape[0]
    rmax = basis.shape[2]
    span = cores.shape[1]
    tile_rows = diag.shape[1]
    my_tile = lax.axis_index("tile")
    my_layer = lax.axis_index("layer")
    row_ids = my_tile * tile_dev + jnp.arange(tile_dev, dtype=jnp.int32)
    col_ids = my_layer * span + jnp.arange(span, dtype=jnp.int32)
    keep = (jnp.arange(rmax, dtype=jnp.int32)[None, :] < ranks[:, None]).astype(jnp.float32)
    masked = basis * keep[:, None, :]
    basis_rows = lax.dynamic_slice_in_dim(masked, my_layer * tile_rows, tile_rows, 1)
    rows_piece = broadcast(diag[0], "tile", 0)
    panel_u = broadcast(masked[0], "tile", 0)
    whole = lax.all_gather(rows_piece, "layer", axis=0, tiled=True)
    lower, solved = factor(whole, panel_u)
    gram = jnp.dot(solved.T, solved, precision=HI)
    lower_rows = lax.dynamic_slice_in_dim(lower, my_layer * tile_rows, tile_rows, 0)
    column = broadcast(cores[:, 0], "layer", 0)
    full_column = lax.all_gather(column, "tile", axis=0, tiled=True)
    others = lax.dynamic_slice_in_dim(full_column, my_layer * span, span, 0)
    coef = jnp.einsum("trs,su->tru", column, gram, precision=HI)
    inner = jnp.einsum("tru,tvu->trv", coef, column, precision=HI)
    partial_rows = jnp.einsum("tar,trv->tav", basis_rows, inner, precision=HI)
    change = jnp.einsum("tav,tbv->tab", partial_rows, masked, precision=HI)
    diag = diag - jnp.where((row_ids > 0)[:, None, None], change, 0.0)
    pair = jnp.einsum("tru,cvu->tcrv", coef, others, precision=HI)
    live = (row_ids[:, None] > col_ids[None, :]) & (col_ids[None, :] > 0)
    cores = cores - jnp.where(live[:, :, None, None], pair, 0.0)
    return (lower_rows[None], solved[None], diag, cores)


def solution(mesh):
    placed = (
        P("tile", None, None),
        P("tile"),
        P("tile", "layer", None, None),
        P("tile", "layer", None),
    )
    return jax.shard_map(
        body,
        mesh=mesh,
        in_specs=placed,
        out_specs=(
            P(None, "layer", None),
            P(),
            P("tile", "layer", None),
            P("tile", "layer", None, None),
        ),
        check_vma=False,
    )
```

profile of v0, /device:TPU:11, one launch (start us, length us, event | category | flops | bytes accessed | tf_op | source)
XLA Modules:
  0.0 164.2 jit_solution(13390756071729577317)
XLA Ops:
  7.2 0.0 copy-start.1
  7.2 0.0 all-reduce.3.cloned.1.call-start
  7.2 1.1 copy.12
  9.0 0.9 select_bitcast_fusion
  9.8 0.8 bitcast_select_fusion
  10.6 0.0 all-reduce.3.cloned.1.call-update
  10.6 0.0 all-gather.2.cloned.1.call-start
  10.7 58.1 %all-reduce.3.cloned.1.call-done = (f32[192,768]{1,0:T(8,128)}, f32[768,32]{1,0:T(8,128)}) async-done(((f32[192,768]{1,0:T(8,128)}, f32[768,32]{1,0:T(8,128)}), (f32[192,768]{1,0:T(8,128)}, f32[768,32]{1,0:T(8,128)})) %all-reduce.3.cloned.1.call-update) | async-done | bytes 688144 | tf_op jit(solution)/shard_map/psum | solution.py:140
  68.8 0.0 all-gather.2.cloned.1.call-update
  68.9 0.0 copy-done.1
  68.9 0.1 copy.13
  69.0 10.3 %psum.23 = f32[1,32,32]{2,1,0:T(8,128)S(1)} all-reduce(f32[1,32,32]{2,1,0:T(8,128)S(1)} %select_bitcast_fusion.1), channel_id=1, replica_groups=mesh['tile'=8,'layer'=4] {'layer'}, use_global_device_ids=true, to_apply=%region_2.3 | all-reduce | flops 1024 | bytes 8192 | tf_op jit(solution)/shard_map/psum | solution.py:140
  79.3 18.9 %all_gather.7 = f32[8,32,32]{2,1,0:T(8,128)S(1)} all-gather(f32[1,32,32]{2,1,0:T(8,128)S(1)} %psum.23), channel_id=1, replica_groups=mesh['tile'=8,'layer'=4] {'tile'}, dimensions={0}, use_global_device_ids=true | all-gather | bytes 36864 | tf_op jit(solution)/shard_map/all_gather | solution.py:162
  98.2 11.0 %all-gather.2.cloned.1.call-done.tile_ref = f32[768,768]{1,0:T(8,128)} async-done(((f32[192,768]{1,0:T(8,128)}), f32[768,768]{1,0:T(8,128)}) %all-gather.2.cloned.1.call-update) | async-done | bytes 2359312 | tf_op jit(solution)/shard_map/all_gather | solution.py:157
  109.2 39.6 %shard_map.75 = (f32[768,768]{1,0:T(8,128)}, f32[768,32]{1,0:T(8,128)}) custom-call(f32[768,768]{1,0:T(8,128)} %all-gather.2.cloned.1.call-done.tile_ref, f32[768,32]{1,0:T(8,128)} %get-tuple-element.17.u_ref), custom_call_target="tpu_custom_call" | custom-call | tf_op jit(solution)/shard_map/pallas_call | solution.py:121
  148.9 1.9 %fusion.17 = f32[32,32]{1,0:T(8,128)S(1)} fusion(f32[768,32]{1,0:T(8,128)} %get-tuple-element.7), kind=kOutput, calls=%fused_computation.26 | convolution fusion | flops 9437184 | bytes 102400 | tf_op jit(solution)/shard_map/dot_general | solution.py:159
  150.8 0.1 fusion.13
  150.9 0.2 fusion.11
  151.1 0.2 fusion.4
  151.3 0.7 copy.15
  152.0 1.8 %copy.14 = f32[1,768,32]{1,2,0:T(8,128)} copy(f32[1,768,32]{2,1,0:T(8,128)} %bitcast.46) | data formatting | bytes 196608
  153.7 1.9 %dynamic-slice_bitcast_fusion = f32[1,192,768]{2,1,0:T(8,128)} fusion(f32[768,768]{1,0:T(8,128)} %get-tuple-element.6, s32[]{:T(128)S(6)} %select_n.64), kind=kLoop, calls=%fused_computation.7 | loop fusion | bytes 1179652 | tf_op jit(solution)/shard_map/broadcast_in_dim | solution.py:172
  155.7 0.2 fusion.6
  155.9 1.5 fusion.1
  (5 shorter events, 0.0 us)
Async XLA Ops:
  7.2 61.7 %copy-start.1 = (f32[1,2,32,32]{3,2,1,0:T(8,128)S(1)}, f32[1,2,32,32]{3,2,1,0:T(8,128)}, u32[]{:S(2)}) copy-start(f32[1,2,32,32]{3,2,1,0:T(8,128)} %param.6) | copy-start | bytes 24580
  7.2 61.7 %all-reduce.3.cloned.1.call-start = ((), (), s32[]{:S(2)}) async-start(), calls=%async_computation.1 | async-start | bytes 1966080 | tf_op jit(solution)/shard_map/psum | solution.py:140
  10.6 98.6 %all-gather.2.cloned.1.call-start = ((), (), s32[]{:S(2)}) async-start(), calls=%async_computation | async-start | bytes 2949120 | tf_op jit(solution)/shard_map/all_gather | solution.py:157
  109.2 46.6 %copy-start = (f32[1,192,768]{2,1,0:T(8,128)S(1)}, f32[1,192,768]{2,1,0:T(8,128)}, u32[]{:S(2)}) copy-start(f32[1,192,768]{2,1,0:T(8,128)} %param.7) | copy-start | bytes 1769476
Sparse Core Ops, SparseCore 0:
  11.0 57.7 all-reduce.2
  70.7 38.5 all-gather.1
where the time goes:
time: 166 us; the launch traced here: 164 us
  waiting for transfers between devices  69.2 us (42%)
  Pallas kernels  39.6 us (24%)
  blocking collectives  29.3 us (18%)
  between operations  14.8 us (9%)
  local copies, waits for them, and re-layouts  5.52 us (3%)
  matrix products  4.05 us (2%)
  other arithmetic  1.68 us (1%)
    psum x1, waiting for transfers between devices, broadcast(): return lax.psum(kept, axis)  58.1 us
    pallas_call x1, Pallas kernels, factor(): pl.pallas_call(chol_kernel, out_shape=(jax.ShapeDtypeStruct((order, order...  39.6 us
    all_gather x1, blocking collectives, body(): full_column = lax.all_gather(column, 'tile', axis=0, tiled=True)  18.9 us
    all_gather x1, waiting for transfers between devices, body(): whole = lax.all_gather(rows_piece, 'layer', axis=0, tiled=True)  11 us
    psum x1, blocking collectives, broadcast(): return lax.psum(kept, axis)  10.3 us
    unnamed x8, local copies, waits for them, and re-layouts  3.6 us
  transfers between devices with their start and end apart: 2, of which 2 were waited for; matrix products, arithmetic and copies ran while one was open for 0% of the time, Pallas kernels for 0%

commit v1 on v0

v1 whole, which is shorter than its diff:
```python
import functools

import jax
import jax.numpy as jnp
from jax import lax
from jax.experimental import pallas as pl
from jax.experimental.pallas import tpu as pltpu
from jax.sharding import PartitionSpec as P

HI = lax.Precision.HIGHEST
B = 128
S = 8


def nt(a, b):
    return lax.dot_general(
        a, b, (((1,), (1,)), ((), ())), precision=HI, preferred_element_type=jnp.float32
    )


def nn(a, b):
    return jnp.dot(a, b, precision=HI, preferred_element_type=jnp.float32)


def total(terms):
    while len(terms) > 1:
        terms = [
            terms[i] + terms[i + 1] if i + 1 < len(terms) else terms[i]
            for i in range(0, len(terms), 2)
        ]
    return terms[0]


def spread_lane(block, lane):
    return jnp.broadcast_to(block[:, lane : lane + 1], (S, B))


def spread_row(block, row):
    return jnp.broadcast_to(block[row : row + 1, :], (S, B))


def base_factor(tile_ref, upper_ref, inv_ref, midway):
    groups = B // S
    sub = lax.broadcasted_iota(jnp.int32, (S, B), 0)
    lane = lax.broadcasted_iota(jnp.int32, (S, B), 1)
    left = [tile_ref[S * g : S * g + S, :] for g in range(groups)]
    right = [jnp.where(lane == sub + S * g, 1.0, 0.0) for g in range(groups)]
    for b in range(groups):
        if b == groups // 2:
            midway()
        a, q = left[b], right[b]
        cols = [spread_lane(a, S * b + j) for j in range(S)]
        e = [[spread_row(cols[j], i) if j <= i else None for j in range(S)] for i in range(S)]
        inv, low = [], [[None] * S for _ in range(S)]
        for j in range(S):
            inv.append(1.0 / e[j][j])
            for i in range(j + 1, S):
                low[i][j] = e[i][j] * inv[j]
            for k in range(j + 1, S):
                for i in range(k, S):
                    e[i][k] = e[i][k] - low[i][j] * e[k][j]
        ra = [spread_row(a, i) for i in range(S)]
        rq = [spread_row(q, i) for i in range(S)]
        for j in range(S):
            for i in range(j + 1, S):
                ra[i] = ra[i] - low[i][j] * ra[j]
                rq[i] = rq[i] - low[i][j] * rq[j]
        xa, xq = None, None
        for j in range(S):
            root = lax.rsqrt(e[j][j])
            ya, yq = ra[j] * root, rq[j] * root
            xa = ya if xa is None else jnp.where(sub == j, ya, xa)
            xq = yq if xq is None else jnp.where(sub == j, yq, xq)
        upper_ref[S * b : S * b + S, :] = jnp.where(lane >= sub + S * b, xa, 0.0)
        inv_ref[S * b : S * b + S, :] = xq
        if b + 1 == groups:
            break
        wa = [ra[j] * inv[j] for j in range(S)]
        wq = [rq[j] * inv[j] for j in range(S)]
        for i in range(S - 1, 0, -1):
            for j in range(i):
                wa[j] = wa[j] - low[i][j] * wa[i]
                wq[j] = wq[j] - low[i][j] * wq[i]
        for g in range(b + 1, groups):
            m = [spread_lane(left[g], S * b + j) for j in range(S)]
            left[g] = left[g] - total([m[j] * wa[j] for j in range(S)])
            right[g] = right[g] - total([m[j] * wq[j] for j in range(S)])


def panel_kernel(
    tiles, layers, diag_ref, masked_ref, masked_t_ref, cores_ref,
    factor_ref, z_ref, diag_out, cores_out,
    work, zt, low, block, upper, inverse, col, oth,
    ztv, send1, recv1, send2, recv2, sendu, recvu, sendc, recvc, sendo, recvo,
):
    t = lax.axis_index("tile")
    l = lax.axis_index("layer")
    rows, order = diag_ref.shape[1], diag_ref.shape[2]
    panels = order // B
    span = cores_ref.shape[1]
    pair_base = t - t % 2
    mine = pl.ds(pl.multiple_of(l * rows, S), rows)
    first = t == 0
    even = t % 2 == 0

    def needed(j, piece):
        return (piece + 1) * rows > j * B

    def remote(src, dst, send, recv, to_t, to_l):
        return pltpu.make_async_remote_copy(
            src_ref=src, dst_ref=dst, send_sem=send, recv_sem=recv,
            device_id=(to_t, to_l), device_id_type=pl.DeviceIdType.MESH,
        )

    def down(j, half):
        return remote(
            diag_ref.at[0, :, pl.ds(pl.multiple_of(j * B, B), B)], work.at[j, mine, :],
            send1.at[half, j], recv1.at[j], 2 * half, l,
        )

    def kept(j):
        return pltpu.make_async_copy(
            diag_ref.at[0, :, pl.ds(pl.multiple_of(j * B, B), B)], work.at[j, mine, :], recv1.at[j]
        )

    def across(j, core, to_l):
        slot = work.at[j, mine, :]
        return remote(slot, slot, send2.at[j, core, to_l], recv2.at[j, l], pair_base + core, to_l)

    def landed(j, piece):
        slot = work.at[j, pl.ds(pl.multiple_of(piece * rows, S), rows), :]
        return remote(slot, slot, send2.at[j, 0, 0], recv2.at[j, piece], t, l)

    def basis_down(half):
        return remote(masked_t_ref, zt, sendu.at[half], recvu, 2 * half, l)

    def basis_kept():
        return pltpu.make_async_copy(masked_t_ref, zt, recvu)

    def basis_across():
        return remote(zt, zt, sendu.at[0], recvu, t + 1, l)

    def column_to(to_l):
        return remote(cores_ref.at[0, 0], col, sendc.at[to_l], recvc, t, to_l)

    def other_to(to_t):
        return remote(
            cores_ref.at[0, 0], oth.at[t % span], sendo.at[to_t], recvo.at[t % span], to_t, t // span
        )

    def each(count, act):
        lax.fori_loop(0, count, lambda i, c: (act(i), c)[1], 0)

    barrier = pltpu.get_barrier_semaphore()
    devices = tiles * layers
    me = t * layers + l

    def greet(i):
        d = lax.rem(me + 1 + i, devices)
        pl.semaphore_signal(
            barrier, inc=1, device_id=(d // layers, d % layers),
            device_id_type=pl.DeviceIdType.MESH,
        )

    @pl.when(first)
    def _():
        each(panels, lambda j: pl.when(needed(j, l))(lambda: kept(j).start()))
        basis_kept().start()

    each(devices - 1, greet)
    pl.semaphore_wait(barrier, devices - 1)

    def relay(j):
        @pl.when(even & needed(j, l))
        def _():
            @pl.when(first)
            def _():
                kept(j).wait()

            @pl.when(jnp.logical_not(first))
            def _():
                down(j, 0).wait_recv()

            def send(i):
                to_l = lax.rem(l + 1 + i, layers)
                across(j, 0, to_l).start()
                across(j, 1, to_l).start()

            across(j, 1, l).start()
            each(layers - 1, send)

    def arrive(j):
        def take(piece):
            @pl.when(needed(j, piece) & (jnp.logical_not(even) | (piece != l)))
            def _():
                landed(j, piece).wait_recv()

        each(layers, take)

    @pl.when(first)
    def _():
        def chunk(j):
            pl.when(needed(j, l))(
                lambda: each(tiles // 2 - 1, lambda h: down(j, tiles // 2 - 1 - h).start())
            )

        chunk(0)
        each(tiles // 2 - 1, lambda h: basis_down(tiles // 2 - 1 - h).start())
        each(panels - 1, lambda j: chunk(j + 1))

    relay(0)

    @pl.when(l == 0)
    def _():
        each(layers - 1, lambda i: column_to(i + 1).start())
        pltpu.make_async_copy(cores_ref.at[0, 0], col, recvc).start()

        def other(i):
            to_t = lax.rem(t + i, tiles)

            @pl.when((to_t != t) | (t // span != 0))
            def _():
                other_to(to_t).start()

        each(tiles, other)

        @pl.when(t // span == 0)
        def _():
            pltpu.make_async_copy(cores_ref.at[0, 0], oth.at[t % span], recvo.at[t % span]).start()

    def basis_relay():
        @pl.when(first)
        def _():
            basis_kept().wait()

        @pl.when(jnp.logical_not(first))
        def _():
            basis_down(0).wait_recv()

        @pl.when(even)
        def _():
            basis_across().start()

    low[...] = jnp.zeros_like(low)

    def panel(k, carry):
        at = pl.ds(pl.multiple_of(k * B, B), B)
        arrive(k)
        for c in range(panels):
            @pl.when(k == c)
            def _():
                here = slice(c * B, c * B + B)
                if c:
                    work2 = work[c, c * B :, :] - nt(low[c * B :, : c * B], low[here, : c * B])
                    low[c * B :, here] = work2
                else:
                    low[:, here] = work[0]
        block[...] = low[at, at]

        def midway():
            @pl.when(k + 1 < panels)
            def _():
                relay(k + 1)

        base_factor(block, upper, inverse, midway)
        low[at, at] = upper[...].T

        @pl.when(k == 0)
        def _():
            basis_relay()
            ztv[...] = zt[...]

        for c in range(panels):
            @pl.when(k == c)
            def _():
                here = slice(c * B, c * B + B)
                rest = slice(c * B + B, order)
                part = ztv[:, here]
                if c:
                    part = part - nt(ztv[:, : c * B], low[here, : c * B])
                ztv[:, here] = nt(part, inverse[...])
                if c + 1 < panels:
                    low[rest, here] = nt(low[rest, here], inverse[...])
        return carry

    lax.fori_loop(0, panels, panel, 0)

    factor_ref[0] = low[mine, :]
    z_ref[0] = ztv[...].T
    gram = nt(ztv[...], ztv[...])

    @pl.when(l == 0)
    def _():
        pltpu.make_async_copy(cores_ref.at[0, 0], col, recvc).wait()

    @pl.when(l != 0)
    def _():
        column_to(0).wait_recv()

    def take_other(s):
        local = (l == 0) & (l * span + s == t)

        @pl.when(local)
        def _():
            pltpu.make_async_copy(cores_ref.at[0, 0], oth.at[s], recvo.at[s]).wait()

        @pl.when(jnp.logical_not(local))
        def _():
            remote(cores_ref.at[0, 0], oth.at[s], sendo.at[0], recvo.at[s], t, l).wait_recv()

    each(span, take_other)
    coef = nn(col[...], gram)
    inner = nt(coef, col[...])
    inner = jnp.where(t > 0, inner, 0.0)
    partial = nn(masked_ref[0, mine, :], inner)
    diag_out[0] = diag_ref[0] - nt(partial, masked_ref[0])
    for s in range(span):
        other_id = l * span + s
        live = (t > other_id) & (other_id > 0)
        cores_out[0, s] = cores_ref[0, s] - jnp.where(live, nt(coef, oth[s]), 0.0)

    @pl.when(first)
    def _():
        def chunk(j):
            pl.when(needed(j, l))(lambda: each(tiles // 2 - 1, lambda h: down(j, h + 1).wait_send()))

        each(panels, chunk)
        each(tiles // 2 - 1, lambda h: basis_down(h + 1).wait_send())

    @pl.when(even)
    def _():
        basis_across().wait_send()

        def chunk(j):
            @pl.when(needed(j, l))
            def _():
                across(j, 1, l).wait_send()

                def sent(i):
                    to_l = lax.rem(l + 1 + i, layers)
                    across(j, 0, to_l).wait_send()
                    across(j, 1, to_l).wait_send()

                each(layers - 1, sent)

        each(panels, chunk)

    @pl.when(l == 0)
    def _():
        each(layers - 1, lambda i: column_to(i + 1).wait_send())

        def other(i):
            to_t = lax.rem(t + i, tiles)

            @pl.when((to_t != t) | (t // span != 0))
            def _():
                other_to(to_t).wait_send()

        each(tiles, other)


def body(tiles, layers, basis, ranks, cores, diag):
    rmax = basis.shape[2]
    span = cores.shape[1]
    rows, order = diag.shape[1], diag.shape[2]
    panels = order // B
    keep = (jnp.arange(rmax, dtype=jnp.int32)[None, :] < ranks[:, None]).astype(jnp.float32)
    masked = basis * keep[:, None, :]
    masked_t = masked[0].T
    vm = pl.BlockSpec(memory_space=pltpu.VMEM)
    f32 = jnp.float32
    dma = pltpu.SemaphoreType.DMA
    return pl.pallas_call(
        functools.partial(panel_kernel, tiles, layers),
        out_shape=(
            jax.ShapeDtypeStruct((1, rows, order), f32),
            jax.ShapeDtypeStruct((1, order, rmax), f32),
            jax.ShapeDtypeStruct(diag.shape, f32),
            jax.ShapeDtypeStruct(cores.shape, f32),
        ),
        in_specs=[vm] * 4,
        out_specs=(vm,) * 4,
        scratch_shapes=[
            pltpu.VMEM((panels, order, B), f32),
            pltpu.VMEM((rmax, order), f32),
            pltpu.VMEM((order, order), f32),
            pltpu.VMEM((B, B), f32),
            pltpu.VMEM((B, B), f32),
            pltpu.VMEM((B, B), f32),
            pltpu.VMEM((rmax, rmax), f32),
            pltpu.VMEM((span, rmax, rmax), f32),
            pltpu.VMEM((rmax, order), f32),
            dma((tiles // 2, panels)),
            dma((panels,)),
            dma((panels, 2, layers)),
            dma((panels, layers)),
            dma((tiles // 2,)),
            dma,
            dma((layers,)),
            dma,
            dma((tiles,)),
            dma((span,)),
        ],
        compiler_params=pltpu.CompilerParams(collective_id=0, has_side_effects=True),
    )(diag, masked, masked_t, cores)


def solution(mesh):
    placed = (
        P("tile", None, None),
        P("tile"),
        P("tile", "layer", None, None),
        P("tile", "layer", None),
    )
    return jax.shard_map(
        functools.partial(body, mesh.shape["tile"], mesh.shape["layer"]),
        mesh=mesh,
        in_specs=placed,
        out_specs=(
            P(None, "layer", None),
            P(),
            P("tile", "layer", None),
            P("tile", "layer", None, None),
        ),
        check_vma=False,
    )
```

time: 166 us -> 74.5 us (0.45)
  waiting for transfers between devices: 69.2 us -> 0 us
  blocking collectives: 29.3 us -> 0 us
  Pallas kernels: 39.6 us -> 65.1 us
  between operations: 14.8 us -> 1.31 us
  matrix products: 4.05 us -> 0 us
    psum x1 -> x0, waiting for transfers between devices: 58.1 us -> none  [broadcast(): return lax.psum(kept, axis)]
    pallas_call x1, Pallas kernels: 39.6 us -> 65.1 us  [body(): pl.pallas_call(functools.partial(panel_kernel, tiles, layers), out_shape=...]
    all_gather x1 -> x0, blocking collectives: 18.9 us -> none  [body(): full_column = lax.all_gather(column, 'tile', axis=0, tiled=True)]
    all_gather x1 -> x0, waiting for transfers between devices: 11 us -> none  [body(): whole = lax.all_gather(rows_piece, 'layer', axis=0, tiled=True)]
    psum x1 -> x0, blocking collectives: 10.3 us -> none  [broadcast(): return lax.psum(kept, axis)]
    dot_general x6 -> x0, matrix products: 4.05 us -> none  [the longest x1 1.88 us: body(): gram = jnp.dot(solved.T, solved, precision=HI)]
    broadcast_in_dim x1 -> x0, local copies, waits for them, and re-layouts: 1.92 us -> none  [body(): return (lower_rows[None], solved[None], diag, cores)]
    pallas_call x0 -> x1, local copies, waits for them, and re-layouts: none -> 1.78 us  [body(): pl.pallas_call(functools.partial(panel_kernel, tiles, layers), out_shape=...]
  transfers between devices with their start and end apart: 2 -> 0, of which waited for: 2 -> 0; matrix products, arithmetic and copies ran while one was open for 0% -> 0% of each run, Pallas kernels for 0% -> 0%
where the time goes in v1:
time: 74.5 us; the launch traced here: 74.3 us
  Pallas kernels  65.1 us (87%)
  local copies, waits for them, and re-layouts  6.12 us (8%)
  other arithmetic  1.75 us (2%)
  between operations  1.31 us (2%)
    pallas_call x1, Pallas kernels, body(): pl.pallas_call(functools.partial(panel_kernel, tiles, layers), out_shape=...  65.1 us
    unnamed x9, local copies, waits for them, and re-layouts  3.42 us
    pallas_call x1, local copies, waits for them, and re-layouts, body(): pl.pallas_call(functools.partial(panel_kernel, tiles, layers), out_shape=...  1.78 us
    transpose x1, other arithmetic, body(): masked_t = masked[0].T  1.67 us

profile of v1, /device:TPU:11, one launch (start us, length us, event | category | flops | bytes accessed | tf_op | source)
XLA Modules:
  0.0 74.3 jit_solution(6980212422756686199)
XLA Ops:
  1.3 0.0 copy-start.1
  1.3 1.7 %fusion.masked_t_ref = f32[32,768]{1,0:T(8,128)} fusion(f32[1,768,32]{1,2,0:T(8,128)} %param.4, f32[32]{0:T(128)S(1)} %compare_convert_fusion), kind=kLoop, calls=%fused_computation.2 | loop fusion | flops 24576 | bytes 196736 | tf_op jit(solution)/shard_map/transpose | solution.py:369
  3.0 0.0 copy-done.1
  3.0 0.1 broadcast_multiply_fusion
  3.1 0.9 %copy.8.masked_ref = f32[1,768,32]{2,1,0:T(8,128)} copy(f32[1,768,32]{1,2,0:T(8,128)S(1)} %broadcast_multiply_fusion) | data formatting | bytes 196608 | tf_op jit(solution)/shard_map/mul | solution.py:368
  4.0 65.1 %shard_map.75 = (f32[1,192,768]{2,1,0:T(8,128)}, f32[1,768,32]{2,1,0:T(8,128)}, f32[1,192,768]{2,1,0:T(8,128)}, f32[1,2,32,32]{3,2,1,0:T(8,128)}) custom-call(f32[1,192,768]{2,1,0:T(8,128)} %diag_ref.1, f32[1,768,32]{2,1,0:T(8,128)} %copy.8.masked_ref, f32[32,768]{1,0:T(8,128)} %fusion.masked_t_ref, f32[1,2,32,32]{3,2,1,0:T(8,128)} %cores_ref.1), custom_call_target="tpu_custom_call" | custom-call | tf_op jit(solution)/shard_map/pallas_call | solution.py:373
  69.1 1.8 %copy.9 = f32[1,768,32]{1,2,0:T(8,128)} copy(f32[1,768,32]{2,1,0:T(8,128)} %get-tuple-element.5) | data formatting | bytes 196608 | tf_op jit(solution)/shard_map/pallas_call | solution.py:373
  70.8 0.0 copy-start
  70.8 2.0 %copy.14 = f32[1,192,768]{2,1,0:T(8,128)} copy(f32[1,192,768]{2,1,0:T(8,128)} %get-tuple-element.12) | data formatting | bytes 1179648
  72.8 0.0 copy-done
  72.8 0.0 copy-start.2
  72.8 0.8 %copy.15 = f32[1,192,768]{2,1,0:T(8,128)} copy(f32[1,192,768]{2,1,0:T(8,128)S(1)} %copy-done) | data formatting | bytes 1179648
  73.6 0.0 copy-done.2
  73.6 0.6 copy.16
  (1 shorter events, 0.0 us)
Async XLA Ops:
  1.3 1.7 %copy-start.1 = (f32[1,768,32]{1,2,0:T(8,128)S(1)}, f32[1,768,32]{1,2,0:T(8,128)}, u32[]{:S(2)}) copy-start(f32[1,768,32]{1,2,0:T(8,128)} %param.4) | copy-start | bytes 294916
  70.8 2.0 %copy-start = (f32[1,192,768]{2,1,0:T(8,128)S(1)}, f32[1,192,768]{2,1,0:T(8,128)}, u32[]{:S(2)}) copy-start(f32[1,192,768]{2,1,0:T(8,128)} %get-tuple-element.14) | copy-start | bytes 1769476
  72.8 0.8 %copy-start.2 = (f32[1,2,32,32]{3,2,1,0:T(8,128)S(1)}, f32[1,2,32,32]{3,2,1,0:T(8,128)}, u32[]{:S(2)}) copy-start(f32[1,2,32,32]{3,2,1,0:T(8,128)} %get-tuple-element.15) | copy-start | bytes 24580

commit v2 on v1

--- a/solution.py
+++ b/solution.py
@@ -35,6 +35,10 @@
     return jnp.broadcast_to(block[:, lane : lane + 1], (S, B))
 
 
+def pick_lane(block, lane):
+    return jnp.take_along_axis(block, jnp.full((S, B), lane, jnp.int32), axis=1)
+
+
 def spread_row(block, row):
     return jnp.broadcast_to(block[row : row + 1, :], (S, B))
 
@@ -44,12 +48,12 @@
     sub = lax.broadcasted_iota(jnp.int32, (S, B), 0)
     lane = lax.broadcasted_iota(jnp.int32, (S, B), 1)
     left = [tile_ref[S * g : S * g + S, :] for g in range(groups)]
-    right = [jnp.where(lane == sub + S * g, 1.0, 0.0) for g in range(groups)]
     for b in range(groups):
         if b == groups // 2:
             midway()
-        a, q = left[b], right[b]
-        cols = [spread_lane(a, S * b + j) for j in range(S)]
+        a = left[b]
+        q = jnp.where(lane < S * b, a, jnp.where(lane == sub + S * b, 1.0, 0.0))
+        cols = [pick_lane(a, S * b + j) for j in range(S)]
         e = [[spread_row(cols[j], i) if j <= i else None for j in range(S)] for i in range(S)]
         inv, low = [], [[None] * S for _ in range(S)]
         for j in range(S):
@@ -75,16 +79,15 @@
         inv_ref[S * b : S * b + S, :] = xq
         if b + 1 == groups:
             break
-        wa = [ra[j] * inv[j] for j in range(S)]
-        wq = [rq[j] * inv[j] for j in range(S)]
+        done = lane < S * b + S
+        w = [jnp.where(done, rq[j], ra[j]) * inv[j] for j in range(S)]
         for i in range(S - 1, 0, -1):
             for j in range(i):
-                wa[j] = wa[j] - low[i][j] * wa[i]
-                wq[j] = wq[j] - low[i][j] * wq[i]
+                w[j] = w[j] - low[i][j] * w[i]
+        pivots = done & (lane >= S * b)
         for g in range(b + 1, groups):
             m = [spread_lane(left[g], S * b + j) for j in range(S)]
-            left[g] = left[g] - total([m[j] * wa[j] for j in range(S)])
-            right[g] = right[g] - total([m[j] * wq[j] for j in range(S)])
+            left[g] = jnp.where(pivots, 0.0, left[g]) - total([m[j] * w[j] for j in range(S)])
 
 
 def panel_kernel(

time: 74.5 us -> 71.7 us (0.962)
  Pallas kernels: 65.1 us -> 62.2 us
    pallas_call x1, Pallas kernels: 65.1 us -> 62.2 us  [body(): pl.pallas_call(functools.partial(panel_kernel, tiles, layers), out_shape=...]
where the time goes in v2:
time: 71.7 us; the launch traced here: 71.4 us
  Pallas kernels  62.2 us (87%)
  local copies, waits for them, and re-layouts  6.12 us (9%)
  other arithmetic  1.75 us (2%)
  between operations  1.31 us (2%)
    pallas_call x1, Pallas kernels, body(): pl.pallas_call(functools.partial(panel_kernel, tiles, layers), out_shape=...  62.2 us
    unnamed x9, local copies, waits for them, and re-layouts  3.42 us
    pallas_call x1, local copies, waits for them, and re-layouts, body(): pl.pallas_call(functools.partial(panel_kernel, tiles, layers), out_shape=...  1.78 us
    transpose x1, other arithmetic, body(): masked_t = masked[0].T  1.67 us

profile of v2, /device:TPU:11, one launch (start us, length us, event | category | flops | bytes accessed | tf_op | source)
XLA Modules:
  0.0 71.4 jit_solution(1664955803004579562)
XLA Ops:
  1.3 0.0 copy-start.1
  1.3 1.7 %fusion.masked_t_ref = f32[32,768]{1,0:T(8,128)} fusion(f32[1,768,32]{1,2,0:T(8,128)} %param.4, f32[32]{0:T(128)S(1)} %compare_convert_fusion), kind=kLoop, calls=%fused_computation.2 | loop fusion | flops 24576 | bytes 196736 | tf_op jit(solution)/shard_map/transpose | solution.py:372
  3.0 0.0 copy-done.1
  3.0 0.1 broadcast_multiply_fusion
  3.1 0.9 %copy.8.masked_ref = f32[1,768,32]{2,1,0:T(8,128)} copy(f32[1,768,32]{1,2,0:T(8,128)S(1)} %broadcast_multiply_fusion) | data formatting | bytes 196608 | tf_op jit(solution)/shard_map/mul | solution.py:371
  4.0 62.2 %shard_map.75 = (f32[1,192,768]{2,1,0:T(8,128)}, f32[1,768,32]{2,1,0:T(8,128)}, f32[1,192,768]{2,1,0:T(8,128)}, f32[1,2,32,32]{3,2,1,0:T(8,128)}) custom-call(f32[1,192,768]{2,1,0:T(8,128)} %diag_ref.1, f32[1,768,32]{2,1,0:T(8,128)} %copy.8.masked_ref, f32[32,768]{1,0:T(8,128)} %fusion.masked_t_ref, f32[1,2,32,32]{3,2,1,0:T(8,128)} %cores_ref.1), custom_call_target="tpu_custom_call" | custom-call | tf_op jit(solution)/shard_map/pallas_call | solution.py:376
  66.2 1.8 %copy.9 = f32[1,768,32]{1,2,0:T(8,128)} copy(f32[1,768,32]{2,1,0:T(8,128)} %get-tuple-element.5) | data formatting | bytes 196608 | tf_op jit(solution)/shard_map/pallas_call | solution.py:376
  68.0 0.0 copy-start
  68.0 2.0 %copy.14 = f32[1,192,768]{2,1,0:T(8,128)} copy(f32[1,192,768]{2,1,0:T(8,128)} %get-tuple-element.12) | data formatting | bytes 1179648
  69.9 0.0 copy-done
  69.9 0.0 copy-start.2
  69.9 0.8 %copy.15 = f32[1,192,768]{2,1,0:T(8,128)} copy(f32[1,192,768]{2,1,0:T(8,128)S(1)} %copy-done) | data formatting | bytes 1179648
  70.8 0.0 copy-done.2
  70.8 0.6 copy.16
  (1 shorter events, 0.0 us)
Async XLA Ops:
  1.3 1.7 %copy-start.1 = (f32[1,768,32]{1,2,0:T(8,128)S(1)}, f32[1,768,32]{1,2,0:T(8,128)}, u32[]{:S(2)}) copy-start(f32[1,768,32]{1,2,0:T(8,128)} %param.4) | copy-start | bytes 294916
  68.0 2.0 %copy-start = (f32[1,192,768]{2,1,0:T(8,128)S(1)}, f32[1,192,768]{2,1,0:T(8,128)}, u32[]{:S(2)}) copy-start(f32[1,192,768]{2,1,0:T(8,128)} %get-tuple-element.14) | copy-start | bytes 1769476
  69.9 0.8 %copy-start.2 = (f32[1,2,32,32]{3,2,1,0:T(8,128)S(1)}, f32[1,2,32,32]{3,2,1,0:T(8,128)}, u32[]{:S(2)}) copy-start(f32[1,2,32,32]{3,2,1,0:T(8,128)} %get-tuple-element.15) | copy-start | bytes 24580

commit v3 on v2

--- a/solution.py
+++ b/solution.py
@@ -10,6 +10,7 @@
 HI = lax.Precision.HIGHEST
 B = 128
 S = 8
+NEAR = 2
 
 
 def nt(a, b):
@@ -20,6 +21,18 @@
 
 def nn(a, b):
     return jnp.dot(a, b, precision=HI, preferred_element_type=jnp.float32)
+
+
+def split(a):
+    high = a.astype(jnp.bfloat16)
+    return high, (a - high.astype(jnp.float32)).astype(jnp.bfloat16)
+
+
+def nn3(a, b):
+    ah, al = split(a)
+    bh, bl = split(b)
+    dot = functools.partial(jnp.dot, preferred_element_type=jnp.float32)
+    return dot(ah, bh) + (dot(ah, bl) + dot(al, bh))
 
 
 def total(terms):
@@ -43,14 +56,12 @@
     return jnp.broadcast_to(block[row : row + 1, :], (S, B))
 
 
-def base_factor(tile_ref, upper_ref, inv_ref, midway):
+def base_factor(tile_ref, upper_ref, inv_ref):
     groups = B // S
     sub = lax.broadcasted_iota(jnp.int32, (S, B), 0)
     lane = lax.broadcasted_iota(jnp.int32, (S, B), 1)
     left = [tile_ref[S * g : S * g + S, :] for g in range(groups)]
     for b in range(groups):
-        if b == groups // 2:
-            midway()
         a = left[b]
         q = jnp.where(lane < S * b, a, jnp.where(lane == sub + S * b, 1.0, 0.0))
         cols = [pick_lane(a, S * b + j) for j in range(S)]
@@ -85,9 +96,19 @@
             for j in range(i):
                 w[j] = w[j] - low[i][j] * w[i]
         pivots = done & (lane >= S * b)
-        for g in range(b + 1, groups):
+        for g in range(b + 1, min(b + 1 + NEAR, groups)):
             m = [spread_lane(left[g], S * b + j) for j in range(S)]
             left[g] = jnp.where(pivots, 0.0, left[g]) - total([m[j] * w[j] for j in range(S)])
+        far = b + 1 + NEAR
+        if far < groups:
+            packed = w[0]
+            for j in range(1, S):
+                packed = jnp.where(sub == j, w[j], packed)
+            rows = [packed if g == b else jnp.zeros((S, B), jnp.float32) for g in range(groups)]
+            moved = nn3(jnp.concatenate(left[far:], axis=0), jnp.concatenate(rows, axis=0))
+            for g in range(far, groups):
+                at = S * (g - far)
+                left[g] = jnp.where(pivots, 0.0, left[g]) - moved[at : at + S, :]
 
 
 def panel_kernel(
@@ -208,8 +229,10 @@
             )
 
         chunk(0)
+        if panels > 1:
+            chunk(1)
         each(tiles // 2 - 1, lambda h: basis_down(tiles // 2 - 1 - h).start())
-        each(panels - 1, lambda j: chunk(j + 1))
+        each(panels - 2, lambda j: chunk(j + 2))
 
     relay(0)
 
@@ -249,6 +272,11 @@
     def panel(k, carry):
         at = pl.ds(pl.multiple_of(k * B, B), B)
         arrive(k)
+
+        @pl.when(k + 1 < panels)
+        def _():
+            relay(k + 1)
+
         for c in range(panels):
             @pl.when(k == c)
             def _():
@@ -260,12 +288,7 @@
                     low[:, here] = work[0]
         block[...] = low[at, at]
 
-        def midway():
-            @pl.when(k + 1 < panels)
-            def _():
-                relay(k + 1)
-
-        base_factor(block, upper, inverse, midway)
+        base_factor(block, upper, inverse)
         low[at, at] = upper[...].T
 
         @pl.when(k == 0)

time: 71.7 us -> 63.7 us (0.89)
  Pallas kernels: 62.2 us -> 54.2 us
    pallas_call x1, Pallas kernels: 62.2 us -> 54.2 us  [body(): pl.pallas_call(functools.partial(panel_kernel, tiles, layers), out_shape=...]
where the time goes in v3:
time: 63.7 us; the launch traced here: 63.4 us
  Pallas kernels  54.2 us (85%)
  local copies, waits for them, and re-layouts  6.12 us (10%)
  other arithmetic  1.75 us (3%)
  between operations  1.31 us (2%)
    pallas_call x1, Pallas kernels, body(): pl.pallas_call(functools.partial(panel_kernel, tiles, layers), out_shape=...  54.2 us
    unnamed x9, local copies, waits for them, and re-layouts  3.42 us
    pallas_call x1, local copies, waits for them, and re-layouts, body(): pl.pallas_call(functools.partial(panel_kernel, tiles, layers), out_shape=...  1.78 us
    transpose x1, other arithmetic, body(): masked_t = masked[0].T  1.67 us

profile of v3, /device:TPU:11, one launch (start us, length us, event | category | flops | bytes accessed | tf_op | source)
XLA Modules:
  0.0 63.4 jit_solution(2601943357705456936)
XLA Ops:
  1.3 0.0 copy-start.1
  1.3 1.7 %fusion.masked_t_ref = f32[32,768]{1,0:T(8,128)} fusion(f32[1,768,32]{1,2,0:T(8,128)} %param.4, f32[32]{0:T(128)S(1)} %compare_convert_fusion), kind=kLoop, calls=%fused_computation.2 | loop fusion | flops 24576 | bytes 196736 | tf_op jit(solution)/shard_map/transpose | solution.py:395
  3.0 0.0 copy-done.1
  3.0 0.1 broadcast_multiply_fusion
  3.1 0.9 %copy.8.masked_ref = f32[1,768,32]{2,1,0:T(8,128)} copy(f32[1,768,32]{1,2,0:T(8,128)S(1)} %broadcast_multiply_fusion) | data formatting | bytes 196608 | tf_op jit(solution)/shard_map/mul | solution.py:394
  4.0 54.2 %shard_map.75 = (f32[1,192,768]{2,1,0:T(8,128)}, f32[1,768,32]{2,1,0:T(8,128)}, f32[1,192,768]{2,1,0:T(8,128)}, f32[1,2,32,32]{3,2,1,0:T(8,128)}) custom-call(f32[1,192,768]{2,1,0:T(8,128)} %diag_ref.1, f32[1,768,32]{2,1,0:T(8,128)} %copy.8.masked_ref, f32[32,768]{1,0:T(8,128)} %fusion.masked_t_ref, f32[1,2,32,32]{3,2,1,0:T(8,128)} %cores_ref.1), custom_call_target="tpu_custom_call" | custom-call | tf_op jit(solution)/shard_map/pallas_call | solution.py:399
  58.2 1.8 %copy.9 = f32[1,768,32]{1,2,0:T(8,128)} copy(f32[1,768,32]{2,1,0:T(8,128)} %get-tuple-element.5) | data formatting | bytes 196608 | tf_op jit(solution)/shard_map/pallas_call | solution.py:399
  60.0 0.0 copy-start
  60.0 2.0 %copy.14 = f32[1,192,768]{2,1,0:T(8,128)} copy(f32[1,192,768]{2,1,0:T(8,128)} %get-tuple-element.12) | data formatting | bytes 1179648
  62.0 0.0 copy-done
  62.0 0.0 copy-start.2
  62.0 0.8 %copy.15 = f32[1,192,768]{2,1,0:T(8,128)} copy(f32[1,192,768]{2,1,0:T(8,128)S(1)} %copy-done) | data formatting | bytes 1179648
  62.8 0.0 copy-done.2
  62.8 0.6 copy.16
  (1 shorter events, 0.0 us)
Async XLA Ops:
  1.3 1.7 %copy-start.1 = (f32[1,768,32]{1,2,0:T(8,128)S(1)}, f32[1,768,32]{1,2,0:T(8,128)}, u32[]{:S(2)}) copy-start(f32[1,768,32]{1,2,0:T(8,128)} %param.4) | copy-start | bytes 294916
  60.0 2.0 %copy-start = (f32[1,192,768]{2,1,0:T(8,128)S(1)}, f32[1,192,768]{2,1,0:T(8,128)}, u32[]{:S(2)}) copy-start(f32[1,192,768]{2,1,0:T(8,128)} %get-tuple-element.14) | copy-start | bytes 1769476
  62.0 0.8 %copy-start.2 = (f32[1,2,32,32]{3,2,1,0:T(8,128)S(1)}, f32[1,2,32,32]{3,2,1,0:T(8,128)}, u32[]{:S(2)}) copy-start(f32[1,2,32,32]{3,2,1,0:T(8,128)} %get-tuple-element.15) | copy-start | bytes 24580

commit v4 on v3

--- a/solution.py
+++ b/solution.py
@@ -7,32 +7,31 @@
 from jax.experimental.pallas import tpu as pltpu
 from jax.sharding import PartitionSpec as P
 
-HI = lax.Precision.HIGHEST
 B = 128
 S = 8
 NEAR = 2
 
 
-def nt(a, b):
-    return lax.dot_general(
-        a, b, (((1,), (1,)), ((), ())), precision=HI, preferred_element_type=jnp.float32
-    )
-
-
-def nn(a, b):
-    return jnp.dot(a, b, precision=HI, preferred_element_type=jnp.float32)
-
-
 def split(a):
     high = a.astype(jnp.bfloat16)
     return high, (a - high.astype(jnp.float32)).astype(jnp.bfloat16)
 
 
-def nn3(a, b):
+def three(a, b, dims):
     ah, al = split(a)
     bh, bl = split(b)
-    dot = functools.partial(jnp.dot, preferred_element_type=jnp.float32)
+    dot = functools.partial(
+        lax.dot_general, dimension_numbers=(dims, ((), ())), preferred_element_type=jnp.float32
+    )
     return dot(ah, bh) + (dot(ah, bl) + dot(al, bh))
+
+
+def nt(a, b):
+    return three(a, b, ((1,), (1,)))
+
+
+def nn(a, b):
+    return three(a, b, ((1,), (0,)))
 
 
 def total(terms):
@@ -105,17 +104,17 @@
             for j in range(1, S):
                 packed = jnp.where(sub == j, w[j], packed)
             rows = [packed if g == b else jnp.zeros((S, B), jnp.float32) for g in range(groups)]
-            moved = nn3(jnp.concatenate(left[far:], axis=0), jnp.concatenate(rows, axis=0))
+            moved = nn(jnp.concatenate(left[far:], axis=0), jnp.concatenate(rows, axis=0))
             for g in range(far, groups):
                 at = S * (g - far)
                 left[g] = jnp.where(pivots, 0.0, left[g]) - moved[at : at + S, :]
 
 
 def panel_kernel(
-    tiles, layers, diag_ref, masked_ref, masked_t_ref, cores_ref,
+    tiles, layers, diag_ref, masked_t_ref, cores_ref,
     factor_ref, z_ref, diag_out, cores_out,
     work, zt, low, block, upper, inverse, col, oth,
-    ztv, send1, recv1, send2, recv2, sendu, recvu, sendc, recvc, sendo, recvo,
+    ztv, own_rows, send1, recv1, send2, recv2, sendu, recvu, sendc, recvc, sendo, recvo,
 ):
     t = lax.axis_index("tile")
     l = lax.axis_index("layer")
@@ -268,6 +267,7 @@
             basis_across().start()
 
     low[...] = jnp.zeros_like(low)
+    own_rows[...] = masked_t_ref[...].T
 
     def panel(k, carry):
         at = pl.ds(pl.multiple_of(k * B, B), B)
@@ -312,7 +312,7 @@
     lax.fori_loop(0, panels, panel, 0)
 
     factor_ref[0] = low[mine, :]
-    z_ref[0] = ztv[...].T
+    z_ref[...] = ztv[...]
     gram = nt(ztv[...], ztv[...])
 
     @pl.when(l == 0)
@@ -338,8 +338,8 @@
     coef = nn(col[...], gram)
     inner = nt(coef, col[...])
     inner = jnp.where(t > 0, inner, 0.0)
-    partial = nn(masked_ref[0, mine, :], inner)
-    diag_out[0] = diag_ref[0] - nt(partial, masked_ref[0])
+    partial = nn(own_rows[mine, :], inner)
+    diag_out[0] = diag_ref[0] - nn(partial, masked_t_ref[...])
     for s in range(span):
         other_id = l * span + s
         live = (t > other_id) & (other_id > 0)
@@ -396,15 +396,15 @@
     vm = pl.BlockSpec(memory_space=pltpu.VMEM)
     f32 = jnp.float32
     dma = pltpu.SemaphoreType.DMA
-    return pl.pallas_call(
+    factors, zt, schur, couplings = pl.pallas_call(
         functools.partial(panel_kernel, tiles, layers),
         out_shape=(
             jax.ShapeDtypeStruct((1, rows, order), f32),
-            jax.ShapeDtypeStruct((1, order, rmax), f32),
+            jax.ShapeDtypeStruct((rmax, order), f32),
             jax.ShapeDtypeStruct(diag.shape, f32),
             jax.ShapeDtypeStruct(cores.shape, f32),
         ),
-        in_specs=[vm] * 4,
+        in_specs=[vm] * 3,
         out_specs=(vm,) * 4,
         scratch_shapes=[
             pltpu.VMEM((panels, order, B), f32),
@@ -416,6 +416,7 @@
             pltpu.VMEM((rmax, rmax), f32),
             pltpu.VMEM((span, rmax, rmax), f32),
             pltpu.VMEM((rmax, order), f32),
+            pltpu.VMEM((order, rmax), f32),
             dma((tiles // 2, panels)),
             dma((panels,)),
             dma((panels, 2, layers)),
@@ -428,7 +429,8 @@
             dma((span,)),
         ],
         compiler_params=pltpu.CompilerParams(collective_id=0, has_side_effects=True),
-    )(diag, masked, masked_t, cores)
+    )(diag, masked_t, cores)
+    return factors, zt.T[None], schur, couplings
 
 
 def solution(mesh):

time: 63.7 us -> 59.5 us (0.934)
  local copies, waits for them, and re-layouts: 6.12 us -> 4.07 us
  Pallas kernels: 54.2 us -> 52.3 us
    pallas_call x1, Pallas kernels: 54.2 us -> 52.3 us  [body(): pl.pallas_call(functools.partial(panel_kernel, tiles, layers), out_shape=...]
    pallas_call x1 -> x0, local copies, waits for them, and re-layouts: 1.78 us -> none  [body(): pl.pallas_call(functools.partial(panel_kernel, tiles, layers), out_shape=...]
    mul x1 -> x0, local copies, waits for them, and re-layouts: 0.92 us -> none  [body(): masked = basis * keep[:, None, :]]
    unnamed x9 -> x10, local copies, waits for them, and re-layouts: 3.42 us -> 4.07 us
where the time goes in v4:
time: 59.5 us; the launch traced here: 59.3 us
  Pallas kernels  52.3 us (88%)
  local copies, waits for them, and re-layouts  4.07 us (7%)
  other arithmetic  1.61 us (3%)
  between operations  1.31 us (2%)
    pallas_call x1, Pallas kernels, body(): pl.pallas_call(functools.partial(panel_kernel, tiles, layers), out_shape=...  52.3 us
    unnamed x10, local copies, waits for them, and re-layouts  4.07 us
    transpose x1, other arithmetic, body(): masked_t = masked[0].T  1.61 us

profile of v4, /device:TPU:11, one launch (start us, length us, event | category | flops | bytes accessed | tf_op | source)
XLA Modules:
  0.0 59.3 jit_solution(18312934246080715421)
XLA Ops:
  1.3 1.6 %multiply_bitcast_fusion.masked_t_ref = f32[32,768]{1,0:T(8,128)} fusion(f32[1,768,32]{1,2,0:T(8,128)} %param.4, f32[32]{0:T(128)S(1)} %compare_convert_fusion), kind=kLoop, calls=%fused_computation | loop fusion | flops 24576 | bytes 196736 | tf_op jit(solution)/shard_map/transpose | solution.py:395
  2.9 52.3 %shard_map.75 = (f32[1,192,768]{2,1,0:T(8,128)}, f32[32,768]{1,0:T(8,128)}, f32[1,192,768]{2,1,0:T(8,128)}, f32[1,2,32,32]{3,2,1,0:T(8,128)}) custom-call(f32[1,192,768]{2,1,0:T(8,128)} %diag_ref.1, f32[32,768]{1,0:T(8,128)} %multiply_bitcast_fusion.masked_t_ref, f32[1,2,32,32]{3,2,1,0:T(8,128)} %cores_ref.1), custom_call_target="tpu_custom_call" | custom-call | tf_op jit(solution)/shard_map/pallas_call | solution.py:399
  55.2 0.0 copy-start.1
  55.2 0.0 copy-start
  55.2 2.0 %copy.13 = f32[1,192,768]{2,1,0:T(8,128)} copy(f32[1,192,768]{2,1,0:T(8,128)} %get-tuple-element.16) | data formatting | bytes 1179648
  57.2 0.0 copy-done.1
  57.2 0.6 %copy.14 = f32[1,768,32]{1,2,0:T(8,128)} copy(f32[1,768,32]{1,2,0:T(8,128)S(1)} %bitcast.9) | data formatting | bytes 196608
  57.8 0.0 copy-done
  57.8 0.0 copy-start.2
  57.8 0.8 %copy.15 = f32[1,192,768]{2,1,0:T(8,128)} copy(f32[1,192,768]{2,1,0:T(8,128)S(1)} %copy-done) | data formatting | bytes 1179648
  58.7 0.0 copy-done.2
  58.7 0.6 %copy.16 = f32[1,2,32,32]{3,2,1,0:T(8,128)} copy(f32[1,2,32,32]{3,2,1,0:T(8,128)S(1)} %copy-done.2) | data formatting | bytes 16384
  (1 shorter events, 0.0 us)
Async XLA Ops:
  55.2 2.0 %copy-start.1 = (f32[32,768]{1,0:T(8,128)S(1)}, f32[32,768]{1,0:T(8,128)}, u32[]{:S(2)}) copy-start(f32[32,768]{1,0:T(8,128)} %get-tuple-element.9) | copy-start | bytes 294916
  55.2 2.6 %copy-start = (f32[1,192,768]{2,1,0:T(8,128)S(1)}, f32[1,192,768]{2,1,0:T(8,128)}, u32[]{:S(2)}) copy-start(f32[1,192,768]{2,1,0:T(8,128)} %get-tuple-element.18) | copy-start | bytes 1769476
  57.8 0.8 %copy-start.2 = (f32[1,2,32,32]{3,2,1,0:T(8,128)S(1)}, f32[1,2,32,32]{3,2,1,0:T(8,128)}, u32[]{:S(2)}) copy-start(f32[1,2,32,32]{3,2,1,0:T(8,128)} %get-tuple-element.19) | copy-start | bytes 24580
